TPU v7x, 32 devices: a whole 2x2x4 slice. The times are simulated.
32 devices in a mesh: groups: 2 (over x), tgt: 16 (over z, y, core).
Axes of the slice: x: 2, y: 2, z: 4, core: 2. Of those that a mesh axis runs over, the one named last changes fastest.
Arguments:
- source_feats: bfloat16 [4096, 1024], P(('groups', 'tgt')), parts along dimension 0, may hold values from -18 to 18
- target_feats: bfloat16 [16384, 1024], P(('groups', 'tgt')), parts along dimension 0, may hold values from -18 to 18
- source_logits: float32 [4096], P('groups'), parts along dimension 0, may hold values from -1.2 to 1.2
- target_logits: float32 [16384], P(('groups', 'tgt')), parts along dimension 0, may hold values from -1 to 3.4
Outputs:
- grad_source: float32 [4096, 1024], P(('groups', 'tgt')), parts along dimension 0
- grad_target: float32 [16384, 1024], P(('groups', 'tgt')), parts along dimension 0
- potential_src: float32 [4096], P('groups'), parts along dimension 0
- potential_tgt: float32 [16384], P(('groups', 'tgt')), parts along dimension 0
There are 2 independent parts, one for each index of `groups`. A program takes and returns all parts, laid end to end along the dimension named above; each array names one. Nothing has to cross between parts.
All inputs are finite; a program needn't handle non-finite values.
Results may differ from a plain program's by a relative error of at most 0.0033.
Values may be sent and summed in bfloat16 or wider, within the bound.
No kernel may reach another device: no remote copies, remote signals or barrier semaphores. Data moves between devices by JAX's collectives and lax.ppermute only.
A program may use at most 64 MiB of HBM per device.

v0:
```python
import math
import jax
import jax.numpy as jnp
from jax import lax
from jax.sharding import PartitionSpec as P

ITERS = 3


def per_device(source_feats, target_feats, source_logits, target_logits):
    width = target_feats.shape[1]
    scale = 1.0 / math.sqrt(width)
    source_count = source_feats.shape[0] * lax.axis_size("tgt")
    target_count = target_feats.shape[0] * lax.axis_size("tgt")
    log_source = source_logits - jnp.log(jnp.sum(jnp.exp(source_logits)))
    target_total = lax.psum(jnp.sum(jnp.exp(target_logits)), "tgt")
    log_target = target_logits - jnp.log(target_total)
    target_sq = jnp.sum(jnp.square(target_feats.astype(jnp.float32)), axis=1)
    gathered = lax.all_gather(source_feats, "tgt", axis=0, tiled=True)
    cross = lax.dot_general(
        gathered, target_feats, (((1,), (1,)), ((), ())), preferred_element_type=jnp.float32
    )
    gathered_sq = jnp.sum(jnp.square(gathered.astype(jnp.float32)), axis=1)
    cost = (gathered_sq[:, None] + target_sq[None, :] - 2.0 * cross) * scale
    potential_tgt = jnp.zeros((target_feats.shape[0],), jnp.float32)
    potential_src = jnp.zeros((source_count,), jnp.float32)
    for step in range(ITERS):
        scores = (log_target + potential_tgt)[None, :] - cost
        top = lax.pmax(jnp.max(scores, axis=1), "tgt")
        total = lax.psum(jnp.sum(jnp.exp(scores - top[:, None]), axis=1), "tgt")
        potential_src = -(top + jnp.log(total))
        column = (log_source + potential_src)[:, None] - cost
        column_top = jnp.max(column, axis=0)
        potential_tgt = -(
            column_top + jnp.log(jnp.sum(jnp.exp(column - column_top[None, :]), axis=0))
        )
    plan = jnp.exp(
        math.log(source_count)
        + (log_source + potential_src)[:, None]
        + (log_target + potential_tgt)[None, :]
        - cost
    ).astype(jnp.bfloat16)
    row_mass = jnp.sum(plan.astype(jnp.float32), axis=1)
    row_part = jnp.dot(plan, target_feats, preferred_element_type=jnp.float32)
    share_part, share_mass = (
        lax.psum_scatter(row_part, "tgt", scatter_dimension=0, tiled=True),
        lax.psum_scatter(row_mass, "tgt", scatter_dimension=0, tiled=True),
    )
    grad_source = share_mass[:, None] * source_feats.astype(jnp.float32) - share_part
    col_part = lax.dot_general(
        plan, gathered, (((0,), (0,)), ((), ())), preferred_element_type=jnp.float32
    )
    col_mass = jnp.sum(plan.astype(jnp.float32), axis=0)
    grad_target = (
        target_count
        / source_count
        * (col_mass[:, None] * target_feats.astype(jnp.float32) - col_part)
    )
    return (grad_source, grad_target, potential_src, potential_tgt)


def solution(mesh):
    return jax.shard_map(
        per_device,
        mesh=mesh,
        in_specs=(
            P(("groups", "tgt"), None),
            P(("groups", "tgt"), None),
            P("groups"),
            P(("groups", "tgt")),
        ),
        out_specs=(
            P(("groups", "tgt"), None),
            P(("groups", "tgt"), None),
            P("groups"),
            P(("groups", "tgt")),
        ),
        check_vma=False,
    )
```

profile of v0, /device:TPU:0, one launch (start us, length us, event | category | flops | bytes accessed | tf_op | source)
XLA Modules:
  0.0 395.1 jit_solution(12551948818565337685)
XLA Ops:
  7.2 0.0 copy-start.5
  7.2 0.0 all-gather.2.cloned.1.call-start
  7.2 0.7 all-gather.2.cloned.1.call-update
  7.9 0.0 reduce-scatter.2.cloned.1.call-start
  8.0 1.3 exponential_reduce_fusion.7
  9.3 36.0 %psum.28 = f32[]{:T(128)} all-reduce(f32[]{:T(128)} %exponential_reduce_fusion.7), channel_id=1, replica_groups=mesh['groups'=2,'tgt'=16] {'tgt'}, use_global_device_ids=true, to_apply=%region_2.0 | all-reduce | flops 1 | bytes 8 | tf_op jit(solution)/shard_map/psum | solution.py:16
  45.9 1.3 exponential_reduce_fusion.6
  47.9 1.5 fusion
  49.5 0.7 broadcast_subtract_fusion
  50.2 13.4 %all-gather.2.cloned.1.call-done = bf16[2048,1024]{1,0:T(8,128)(2,1)} async-done(((bf16[128,1024]{1,0:T(8,128)(2,1)}), bf16[2048,1024]{1,0:T(8,128)(2,1)}) %all-gather.2.cloned.1.call-update) | async-done | bytes 4194320 | tf_op jit(solution)/shard_map/all_gather | solution.py:19
  63.6 3.2 multiply_reduce_fusion
  66.8 0.2 copy-done.3
  67.0 4.8 %subtract_reduce_fusion.5 = (f32[2048]{0:T(1024)S(1)}, f32[2048,512]{1,0:T(8,128)}) fusion(f32[512]{0:T(512)S(1)} %broadcast_subtract_fusion, bf16[2048,1024]{1,0:T(8,128)(2,1)S(1)} %copy-done.3, bf16[512,1024]{1,0:T(8,128)(2,1)S(1)} %copy-done.5, f32[512]{0:T(512)S(1)} %fusion, f32[2048]{0:T(1024)S(1)} %multiply_reduce_fusion), kind=kOutput, calls=%fused_computation.16 | convolution fusion | flops 2153773056 | bytes 9457664 | tf_op jit(solution)/shard_map/dot_general | solution.py:20
  71.8 31.6 %pmax.21 = f32[2048]{0:T(1024)S(1)} all-reduce(f32[2048]{0:T(1024)S(1)} %get-tuple-element.12), channel_id=1, replica_groups=mesh['groups'=2,'tgt'=16] {'tgt'}, use_global_device_ids=true, to_apply=%region_6.0 | all-reduce | flops 2048 | bytes 16384 | tf_op jit(solution)/shard_map/pmax | solution.py:29
  103.5 3.2 exponential_reduce_fusion.5
  106.7 30.0 %psum.29 = f32[2048]{0:T(1024)S(1)} all-reduce(f32[2048]{0:T(1024)S(1)} %exponential_reduce_fusion.5), channel_id=1, replica_groups=mesh['groups'=2,'tgt'=16] {'tgt'}, use_global_device_ids=true, to_apply=%region_8.0 | all-reduce | flops 2048 | bytes 16384 | tf_op jit(solution)/shard_map/psum | solution.py:30
  136.7 0.0 copy-done.6
  136.7 0.0 copy-start
  136.7 0.0 copy-start.7
  136.8 2.7 subtract_reduce_fusion.4
  139.4 0.7 copy-done
  140.2 0.8 exponential_reduce_fusion.4
  141.0 0.4 subtract_reduce_fusion.3
  141.3 30.0 %pmax.22 = f32[2048]{0:T(1024)S(1)} all-reduce(f32[2048]{0:T(1024)S(1)} %subtract_reduce_fusion.3), channel_id=1, replica_groups=mesh['groups'=2,'tgt'=16] {'tgt'}, use_global_device_ids=true, to_apply=%region_12.0 | all-reduce | flops 2048 | bytes 16384 | tf_op jit(solution)/shard_map/pmax | solution.py:29
  171.3 3.2 exponential_reduce_fusion.3
  174.5 30.0 %psum.30 = f32[2048]{0:T(1024)S(1)} all-reduce(f32[2048]{0:T(1024)S(1)} %exponential_reduce_fusion.3), channel_id=1, replica_groups=mesh['groups'=2,'tgt'=16] {'tgt'}, use_global_device_ids=true, to_apply=%region_14.0 | all-reduce | flops 2048 | bytes 16384 | tf_op jit(solution)/shard_map/psum | solution.py:30
  204.5 0.0 copy-start.1
  204.6 2.7 subtract_reduce_fusion.2
  207.3 0.7 copy-done.1
  208.0 0.8 exponential_reduce_fusion.2
  208.8 0.4 subtract_reduce_fusion.1
  209.1 30.0 %pmax.23 = f32[2048]{0:T(1024)S(1)} all-reduce(f32[2048]{0:T(1024)S(1)} %subtract_reduce_fusion.1), channel_id=1, replica_groups=mesh['groups'=2,'tgt'=16] {'tgt'}, use_global_device_ids=true, to_apply=%region_18.0 | all-reduce | flops 2048 | bytes 16384 | tf_op jit(solution)/shard_map/pmax | solution.py:29
  239.1 3.2 exponential_reduce_fusion.1
  242.3 30.2 %psum.31 = f32[2048]{0:T(1024)S(1)} all-reduce(f32[2048]{0:T(1024)S(1)} %exponential_reduce_fusion.1), channel_id=1, replica_groups=mesh['groups'=2,'tgt'=16] {'tgt'}, use_global_device_ids=true, to_apply=%region_20.0 | all-reduce | flops 2048 | bytes 16384 | tf_op jit(solution)/shard_map/psum | solution.py:30
  272.5 0.6 broadcast_add_fusion
  273.1 2.9 subtract_reduce_fusion
  276.0 0.8 exponential_reduce_fusion
  276.8 0.6 fusion.3
  277.4 1.3 convert_reduce_fusion
  278.7 5.6 %fusion.4 = f32[2048,1024]{1,0:T(8,128)} fusion(bf16[2048,512]{1,0:T(8,128)(2,1)S(1)} %get-tuple-element.6, bf16[512,1024]{1,0:T(8,128)(2,1)S(1)} %copy-done.5), kind=kOutput, calls=%fused_computation.35 | convolution fusion | flops 2147483648 | bytes 11534336 | tf_op jit(solution)/shard_map/dot_general | solution.py:44
  284.3 0.0 reduce-scatter.2.cloned.1.call-update
  284.3 0.6 copy-done.8
  284.9 0.6 dynamic-slice
  286.2 30.1 %all-reduce = f32[2048]{0:T(1024)S(1)} all-reduce(f32[2048]{0:T(1024)S(1)} %get-tuple-element.5), channel_id=2, replica_groups=mesh['groups'=2,'tgt'=16] {'tgt'}, use_global_device_ids=true, to_apply=%region_24.0.clone | all-reduce | flops 2048 | bytes 16384
  316.3 0.1 dynamic-slice.1
  316.3 5.9 %fusion.2 = f32[512,1024]{1,0:T(8,128)} fusion(bf16[512,1024]{1,0:T(8,128)(2,1)S(1)} %copy-done.5, bf16[2048,512]{1,0:T(8,128)(2,1)S(1)} %get-tuple-element.6, bf16[2048,1024]{1,0:T(8,128)(2,1)} %all-gather.2.cloned.1.call-done, f32[512]{0:T(512)S(1)} %get-tuple-element.4), kind=kOutput, calls=%fused_computation.21 | convolution fusion | flops 2149580800 | bytes 9439232 | tf_op jit(solution)/shard_map/dot_general | solution.py:50
  322.2 64.0 %reduce-scatter.2.cloned.1.call-done = f32[128,1024]{1,0:T(8,128)} async-done(((f32[2048,1024]{1,0:T(8,128)}), f32[128,1024]{1,0:T(8,128)}) %reduce-scatter.2.cloned.1.call-update) | async-done | bytes 524304 | tf_op jit(solution)/shard_map/reduce_scatter | solution.py:46
  386.3 2.0 multiply_subtract_fusion
  (13 shorter events, 0.1 us)
Async XLA Ops:
  7.2 59.6 %copy-start.5 = (bf16[512,1024]{1,0:T(8,128)(2,1)S(1)}, bf16[512,1024]{1,0:T(8,128)(2,1)}, u32[]{:S(2)}) copy-start(bf16[512,1024]{1,0:T(8,128)(2,1)} %param.5) | copy-start | bytes 3145732
  7.2 56.4 %all-gather.2.cloned.1.call-start = ((), (), s32[]{:S(2)}) async-start(), calls=%async_computation.1 | async-start | bytes 4456448 | tf_op jit(solution)/shard_map/all_gather | solution.py:19
  7.9 378.4 %reduce-scatter.2.cloned.1.call-start = ((), (), s32[]{:S(2)}) async-start(), calls=%async_computation.2 | async-start | bytes 8912896 | tf_op jit(solution)/shard_map/reduce_scatter | solution.py:46
  63.6 3.4 copy-start.3
  71.8 64.9 %copy-start.6 = (f32[2048]{0:T(1024)S(1)}, f32[2048]{0:T(1024)}, u32[]{:S(2)}) copy-start(f32[2048]{0:T(1024)} %param.6) | copy-start | bytes 24580
  136.7 3.5 copy-start
  136.7 4.2 %copy-start.7 = (f32[512]{0:T(512)S(1)}, f32[512]{0:T(512)}, u32[]{:S(2)}) copy-start(f32[512]{0:T(512)} %param.7) | copy-start | bytes 6148
  204.5 3.5 copy-start.1
  272.5 3.5 copy-start.2
  284.3 0.7 copy-start.8
  316.3 69.9 %copy-start.4 = (bf16[128,1024]{1,0:T(8,128)(2,1)S(1)}, bf16[128,1024]{1,0:T(8,128)(2,1)}, u32[]{:S(2)}) copy-start(bf16[128,1024]{1,0:T(8,128)(2,1)} %param.4) | copy-start | bytes 786436
Sparse Core Ops, SparseCore 0:
  10.2 53.3 all-gather.1
  284.4 101.8 reduce-scatter.1
where the time goes:
time: 396 us; the launch traced here: 395 us
  blocking collectives  248 us (63%)
  waiting for transfers between devices  78.1 us (20%)
  other arithmetic  33.4 us (8%)
  matrix products  16.3 us (4%)
  between operations  16.3 us (4%)
    pmax x3, blocking collectives, per_device(): top = lax.pmax(jnp.max(scores, axis=1), 'tgt')  91.6 us
    psum x3, blocking collectives, per_device(): total = lax.psum(jnp.sum(jnp.exp(scores - top[:, None]), axis=1), 'tgt')  90.2 us
    reduce_scatter x1, waiting for transfers between devices, per_device(): lax.psum_scatter(row_part, 'tgt', scatter_dimension=0, tiled=True)  64 us
    psum x1, blocking collectives, per_device(): target_total = lax.psum(jnp.sum(jnp.exp(target_logits)), 'tgt')  36 us
    unnamed x1, blocking collectives  30.1 us
    all_gather x1, waiting for transfers between devices, per_device(): gathered = lax.all_gather(source_feats, 'tgt', axis=0, tiled=True)  13.4 us
    reduce_sum x3, other arithmetic, per_device(): total = lax.psum(jnp.sum(jnp.exp(scores - top[:, None]), axis=1), 'tgt')  9.62 us
    reduce_max x3, other arithmetic, per_device(): column_top = jnp.max(column, axis=0)  8.23 us
  transfers between devices with their start and end apart: 2, of which 2 were waited for; matrix products, arithmetic and copies ran while one was open for 3% of the time, Pallas kernels for 0%

commit v1 on v0

--- a/solution.py
+++ b/solution.py
@@ -27,7 +27,9 @@
     for step in range(ITERS):
         scores = (log_target + potential_tgt)[None, :] - cost
         top = lax.pmax(jnp.max(scores, axis=1), "tgt")
-        total = lax.psum(jnp.sum(jnp.exp(scores - top[:, None]), axis=1), "tgt")
+        total = jnp.sum(
+            lax.all_gather(jnp.sum(jnp.exp(scores - top[:, None]), axis=1), "tgt"), axis=0
+        )
         potential_src = -(top + jnp.log(total))
         column = (log_source + potential_src)[:, None] - cost
         column_top = jnp.max(column, axis=0)

time: 396 us -> 364 us (0.919)
  blocking collectives: 248 us -> 216 us
    psum x3 -> x0, blocking collectives: 90.2 us -> none  [per_device(): total = lax.psum(jnp.sum(jnp.exp(scores - top[:, None]), axis=1), 'tgt')]
    all_gather x0 -> x3, blocking collectives: none -> 52.7 us  [per_device(): lax.all_gather(jnp.sum(jnp.exp(scores - top[:, None]), axis=1), 'tgt')]
    reduce_sum x3 -> x6, other arithmetic: 9.62 us -> 9.68 us  [the longest x3 9.6 us: per_device(): jnp.sum(jnp.exp(scores - top[:, None]), axis=1)]
where the time goes in v1:
time: 364 us; the launch traced here: 363 us
  blocking collectives  216 us (59%)
  waiting for transfers between devices  77.6 us (21%)
  other arithmetic  33.5 us (9%)
  matrix products  16.3 us (4%)
  between operations  16.3 us (4%)
    pmax x3, blocking collectives, per_device(): top = lax.pmax(jnp.max(scores, axis=1), 'tgt')  95.5 us
    reduce_scatter x1, waiting for transfers between devices, per_device(): lax.psum_scatter(row_part, 'tgt', scatter_dimension=0, tiled=True)  63.5 us
    all_gather x3, blocking collectives, per_device(): lax.all_gather(jnp.sum(jnp.exp(scores - top[:, None]), axis=1), 'tgt')  52.7 us
    psum x1, blocking collectives, per_device(): target_total = lax.psum(jnp.sum(jnp.exp(target_logits)), 'tgt')  36 us
    unnamed x1, blocking collectives  32 us
    all_gather x1, waiting for transfers between devices, per_device(): gathered = lax.all_gather(source_feats, 'tgt', axis=0, tiled=True)  13.4 us
    reduce_sum x3, other arithmetic, per_device(): jnp.sum(jnp.exp(scores - top[:, None]), axis=1)  9.6 us
    reduce_max x3, other arithmetic, per_device(): column_top = jnp.max(column, axis=0)  8.23 us
  transfers between devices with their start and end apart: 2, of which 2 were waited for; matrix products, arithmetic and copies ran while one was open for 3% of the time, Pallas kernels for 0%

profile of v1, /device:TPU:0, one launch (start us, length us, event | category | flops | bytes accessed | tf_op | source)
XLA Modules:
  0.0 363.1 jit_solution(6604175976844115843)
XLA Ops:
  7.2 0.0 copy-start.5
  7.2 0.0 all-gather.5.cloned.1.call-start
  7.2 0.7 all-gather.5.cloned.1.call-update
  7.9 0.0 reduce-scatter.2.cloned.1.call-start
  8.0 1.3 exponential_reduce_fusion.7
  9.3 36.0 %psum.7 = f32[]{:T(128)} all-reduce(f32[]{:T(128)} %exponential_reduce_fusion.7), channel_id=1, replica_groups=mesh['groups'=2,'tgt'=16] {'tgt'}, use_global_device_ids=true, to_apply=%region_2.0 | all-reduce | flops 1 | bytes 8 | tf_op jit(solution)/shard_map/psum | solution.py:16
  45.9 1.3 exponential_reduce_fusion.6
  47.9 1.5 fusion
  49.5 0.7 broadcast_subtract_fusion
  50.2 13.4 %all-gather.5.cloned.1.call-done = bf16[2048,1024]{1,0:T(8,128)(2,1)} async-done(((bf16[128,1024]{1,0:T(8,128)(2,1)}), bf16[2048,1024]{1,0:T(8,128)(2,1)}) %all-gather.5.cloned.1.call-update) | async-done | bytes 4194320 | tf_op jit(solution)/shard_map/all_gather | solution.py:19
  63.6 3.2 multiply_reduce_fusion
  66.8 0.0 copy-done.5
  66.8 0.2 copy-done.3
  67.0 4.8 %subtract_reduce_fusion.5 = (f32[2048]{0:T(1024)S(1)}, f32[2048,512]{1,0:T(8,128)}) fusion(f32[512]{0:T(512)S(1)} %broadcast_subtract_fusion, bf16[2048,1024]{1,0:T(8,128)(2,1)S(1)} %copy-done.3, bf16[512,1024]{1,0:T(8,128)(2,1)S(1)} %copy-done.5, f32[512]{0:T(512)S(1)} %fusion, f32[2048]{0:T(1024)S(1)} %multiply_reduce_fusion), kind=kOutput, calls=%fused_computation.16 | convolution fusion | flops 2153773056 | bytes 9457664 | tf_op jit(solution)/shard_map/dot_general | solution.py:20
  71.8 31.6 %pmax.21 = f32[2048]{0:T(1024)S(1)} all-reduce(f32[2048]{0:T(1024)S(1)} %get-tuple-element.12), channel_id=1, replica_groups=mesh['groups'=2,'tgt'=16] {'tgt'}, use_global_device_ids=true, to_apply=%region_6.0 | all-reduce | flops 2048 | bytes 16384 | tf_op jit(solution)/shard_map/pmax | solution.py:29
  103.5 3.2 exponential_reduce_fusion.5
  106.7 17.5 %all-gather = f32[32768]{0:T(1024)S(1)} all-gather(f32[2048]{0:T(1024)S(1)} %exponential_reduce_fusion.5), channel_id=2, replica_groups=mesh['groups'=2,'tgt'=16] {'tgt'}, dimensions={0}, use_global_device_ids=true | all-gather | bytes 139264 | tf_op jit(solution)/shard_map/all_gather | solution.py:31
  124.2 0.0 copy-done.6
  124.3 0.0 copy-start
  124.3 0.0 copy-start.7
  124.3 2.7 subtract_reduce_fusion.4
  127.0 0.7 copy-done
  127.7 0.8 exponential_reduce_fusion.4
  128.5 0.4 subtract_reduce_fusion.3
  128.9 31.9 %pmax.22 = f32[2048]{0:T(1024)S(1)} all-reduce(f32[2048]{0:T(1024)S(1)} %subtract_reduce_fusion.3), channel_id=1, replica_groups=mesh['groups'=2,'tgt'=16] {'tgt'}, use_global_device_ids=true, to_apply=%region_12.0 | all-reduce | flops 2048 | bytes 16384 | tf_op jit(solution)/shard_map/pmax | solution.py:29
  160.8 3.2 exponential_reduce_fusion.3
  164.0 17.5 %all-gather.1 = f32[32768]{0:T(1024)S(1)} all-gather(f32[2048]{0:T(1024)S(1)} %exponential_reduce_fusion.3), channel_id=3, replica_groups=mesh['groups'=2,'tgt'=16] {'tgt'}, dimensions={0}, use_global_device_ids=true | all-gather | bytes 139264 | tf_op jit(solution)/shard_map/all_gather | solution.py:31
  181.6 2.7 subtract_reduce_fusion.2
  184.3 0.7 copy-done.1
  185.0 0.8 exponential_reduce_fusion.2
  185.8 0.4 subtract_reduce_fusion.1
  186.2 31.9 %pmax.23 = f32[2048]{0:T(1024)S(1)} all-reduce(f32[2048]{0:T(1024)S(1)} %subtract_reduce_fusion.1), channel_id=1, replica_groups=mesh['groups'=2,'tgt'=16] {'tgt'}, use_global_device_ids=true, to_apply=%region_18.0 | all-reduce | flops 2048 | bytes 16384 | tf_op jit(solution)/shard_map/pmax | solution.py:29
  218.1 3.2 exponential_reduce_fusion.1
  221.3 17.7 %all-gather.2 = f32[32768]{0:T(1024)S(1)} all-gather(f32[2048]{0:T(1024)S(1)} %exponential_reduce_fusion.1), channel_id=4, replica_groups=mesh['groups'=2,'tgt'=16] {'tgt'}, dimensions={0}, use_global_device_ids=true | all-gather | bytes 139264 | tf_op jit(solution)/shard_map/all_gather | solution.py:31
  239.1 0.6 broadcast_add_fusion
  239.7 2.8 subtract_reduce_fusion
  242.6 0.8 exponential_reduce_fusion
  243.3 0.6 fusion.3
  243.9 1.3 convert_reduce_fusion
  245.3 5.6 %fusion.4 = f32[2048,1024]{1,0:T(8,128)} fusion(bf16[2048,512]{1,0:T(8,128)(2,1)S(1)} %get-tuple-element.6, bf16[512,1024]{1,0:T(8,128)(2,1)S(1)} %copy-done.5), kind=kOutput, calls=%fused_computation.35 | convolution fusion | flops 2147483648 | bytes 11534336 | tf_op jit(solution)/shard_map/dot_general | solution.py:46
  250.8 0.0 reduce-scatter.2.cloned.1.call-update
  250.9 0.6 copy-done.8
  251.5 0.6 dynamic-slice
  252.7 32.0 %all-reduce = f32[2048]{0:T(1024)S(1)} all-reduce(f32[2048]{0:T(1024)S(1)} %get-tuple-element.5), channel_id=5, replica_groups=mesh['groups'=2,'tgt'=16] {'tgt'}, use_global_device_ids=true, to_apply=%region_24.0.clone | all-reduce | flops 2048 | bytes 16384
  284.8 0.1 dynamic-slice.1
  284.8 5.9 %fusion.2 = f32[512,1024]{1,0:T(8,128)} fusion(bf16[512,1024]{1,0:T(8,128)(2,1)S(1)} %copy-done.5, bf16[2048,512]{1,0:T(8,128)(2,1)S(1)} %get-tuple-element.6, bf16[2048,1024]{1,0:T(8,128)(2,1)} %all-gather.5.cloned.1.call-done, f32[512]{0:T(512)S(1)} %get-tuple-element.4), kind=kOutput, calls=%fused_computation.21 | convolution fusion | flops 2149580800 | bytes 9439232 | tf_op jit(solution)/shard_map/dot_general | solution.py:52
  290.7 63.5 %reduce-scatter.2.cloned.1.call-done = f32[128,1024]{1,0:T(8,128)} async-done(((f32[2048,1024]{1,0:T(8,128)}), f32[128,1024]{1,0:T(8,128)}) %reduce-scatter.2.cloned.1.call-update) | async-done | bytes 524304 | tf_op jit(solution)/shard_map/reduce_scatter | solution.py:48
  354.3 2.0 multiply_subtract_fusion
  (19 shorter events, 0.2 us)
Async XLA Ops:
  7.2 59.6 %copy-start.5 = (bf16[512,1024]{1,0:T(8,128)(2,1)S(1)}, bf16[512,1024]{1,0:T(8,128)(2,1)}, u32[]{:S(2)}) copy-start(bf16[512,1024]{1,0:T(8,128)(2,1)} %param.5) | copy-start | bytes 3145732
  7.2 56.4 %all-gather.5.cloned.1.call-start = ((), (), s32[]{:S(2)}) async-start(), calls=%async_computation.1 | async-start | bytes 4456448 | tf_op jit(solution)/shard_map/all_gather | solution.py:19
  7.9 346.4 %reduce-scatter.2.cloned.1.call-start = ((), (), s32[]{:S(2)}) async-start(), calls=%async_computation.2 | async-start | bytes 8912896 | tf_op jit(solution)/shard_map/reduce_scatter | solution.py:48
  63.6 3.4 copy-start.3
  71.8 52.4 %copy-start.6 = (f32[2048]{0:T(1024)S(1)}, f32[2048]{0:T(1024)}, u32[]{:S(2)}) copy-start(f32[2048]{0:T(1024)} %param.6) | copy-start | bytes 24580
  124.3 3.5 copy-start
  124.3 4.2 %copy-start.7 = (f32[512]{0:T(512)S(1)}, f32[512]{0:T(512)}, u32[]{:S(2)}) copy-start(f32[512]{0:T(512)} %param.7) | copy-start | bytes 6148
  181.6 3.5 copy-start.1
  239.1 3.5 copy-start.2
  250.8 0.7 copy-start.8
  284.8 69.4 %copy-start.4 = (bf16[128,1024]{1,0:T(8,128)(2,1)S(1)}, bf16[128,1024]{1,0:T(8,128)(2,1)}, u32[]{:S(2)}) copy-start(bf16[128,1024]{1,0:T(8,128)(2,1)} %param.4) | copy-start | bytes 786436
Sparse Core Ops, SparseCore 0:
  10.2 53.3 all-gather.4
  251.0 103.2 reduce-scatter.1
